TPU v7x, 32 devices: a whole 2x2x4 slice. The times are simulated.
32 devices in a mesh: ctx: 8 (over z, y), head: 4 (over x, core).
Axes of the slice: x: 2, y: 2, z: 4, core: 2. Of those that a mesh axis runs over, the one named last changes fastest.
Arguments:
- queries: bfloat16 [1024, 64, 128], P('ctx', 'head'), may hold values from -90 to 90
- key_states: bfloat16 [1024, 8, 128], P('ctx', 'head'), may hold values from -4.5 to 4.5
- value_states: bfloat16 [1024, 8, 128], P('ctx', 'head'), may hold values from -6 to 6
- chosen: int32 [2, 4], replicated, may hold values from 0 to 1, as said below
- valid_count: int32 [2], replicated, may hold values from 1 to 2, as said below
Outputs:
- attn_out: bfloat16 [1024, 64, 128], P('ctx', 'head')
- key_mass: float32 [64, 1024], P('head', 'ctx')
Inputs may be any that keep to these rules, and one draw needn't show every extreme that they name: `chosen`: row i lists block i first; if valid_count[i] >= 2, block 0 second; the next valid_count[i] - 2 entries are distinct blocks from 1 to i - 1; entries from position valid_count[i] on equal i. valid_count[i] is at most min(4, i + 1), and the last block's count is min(4, 2).
All inputs are finite; a program needn't handle non-finite values.
Results may differ from a plain program's by a relative error of at most 0.0046.
Values may be sent and summed in bfloat16 or wider, within the bound.
A program may use at most 64 MiB of HBM per device.

v0:
```python
import math
import jax
import jax.numpy as jnp
from jax import lax
from jax.sharding import PartitionSpec as P

BLOCK = 512


def from_partner(value, axis, bit):
    mask = 2**bit
    pairs = [(source, source ^ mask) for source in range(lax.axis_size(axis))]
    return lax.ppermute(value, axis, pairs)


def on_device(queries, key_states, value_states, chosen, valid_count):
    ctx_size = lax.axis_size("ctx")
    my_index = lax.axis_index("ctx")
    token_count = queries.shape[0]
    query_heads = queries.shape[1]
    head_depth = queries.shape[2]
    kv_total = key_states.shape[1]
    groups = query_heads // kv_total
    slot_total = chosen.shape[1]
    split_count = BLOCK // token_count
    quarter = token_count // split_count
    my_block = my_index // split_count
    my_member = my_index % split_count
    listed = chosen[my_block]
    slot_ids = jnp.arange(slot_total)
    slot_valid = slot_ids < valid_count[my_block]
    owners = jnp.arange(ctx_size) // split_count
    wanted = jnp.any(
        (slot_ids[None, :] < valid_count[owners][:, None]) & (chosen[owners] == my_block), axis=1
    )
    stacked = jnp.stack([key_states, value_states]).reshape(
        2, 1, split_count, quarter, kv_total, head_depth
    )
    outgoing = jnp.broadcast_to(
        stacked, (2, ctx_size // split_count, split_count, quarter, kv_total, head_depth)
    )
    outgoing = outgoing.reshape(2, ctx_size, quarter, kv_total, head_depth)
    outgoing = jnp.where(wanted[None, :, None, None, None], outgoing, jnp.zeros((), outgoing.dtype))
    incoming = lax.all_to_all(outgoing, "ctx", split_axis=1, concat_axis=1, tiled=True)
    sources = (listed[:, None] * split_count + jnp.arange(split_count)[None, :]).reshape(-1)
    fetched = jnp.take(incoming, sources, axis=1)
    bit_total = split_count.bit_length() - 1
    for bit_index in range(bit_total):
        partner = from_partner(fetched, "ctx", bit_index)
        is_lower = my_member // 2**bit_index % 2 == 0
        fetched = jnp.where(
            is_lower,
            jnp.concatenate([fetched, partner], axis=2),
            jnp.concatenate([partner, fetched], axis=2),
        )
    fetched = fetched.reshape(2, slot_total * BLOCK, kv_total, head_depth)
    by_head = jnp.transpose(fetched, (0, 2, 1, 3))
    query_pos = my_index * token_count + jnp.arange(token_count)
    score_scale = 1.0 / math.sqrt(head_depth)
    grouped = queries.reshape(token_count, kv_total, groups, head_depth)
    offsets = jnp.arange(BLOCK)
    key_pos = (listed[:, None] * BLOCK + offsets[None, :]).reshape(-1)
    key_block = jnp.repeat(listed, BLOCK)
    key_valid = jnp.repeat(slot_valid, BLOCK)
    visibility = key_valid[None, :] & (
        (key_block[None, :] < my_block) | (key_pos[None, :] <= query_pos[:, None])
    )
    contract_last = (((1,), (1,)), ((), ()))
    head_outputs = []
    head_masses = []
    for kv_head in range(kv_total):
        key_head = by_head[0, kv_head]
        value_head = by_head[1, kv_head]
        for group_index in range(groups):
            raw_scores = (
                lax.dot_general(
                    grouped[:, kv_head, group_index],
                    key_head,
                    contract_last,
                    preferred_element_type=jnp.float32,
                )
                * score_scale
            )
            scores = jnp.where(visibility, raw_scores, -jnp.inf)
            highest = jnp.max(scores, axis=-1, keepdims=True)
            raised = jnp.exp(scores - highest)
            attention = raised / jnp.sum(raised, axis=-1, keepdims=True)
            head_outputs.append(
                jnp.dot(
                    attention.astype(jnp.bfloat16), value_head, preferred_element_type=jnp.float32
                )
            )
            head_masses.append(jnp.sum(attention, axis=0).reshape(slot_total, BLOCK))
    attn_out = jnp.stack(head_outputs, axis=1).astype(jnp.bfloat16)
    contrib = jnp.stack(head_masses, axis=1).reshape(
        slot_total, query_heads, split_count, token_count
    )
    contrib = jnp.transpose(contrib, (0, 2, 1, 3)).reshape(
        slot_total * split_count, query_heads, token_count
    )
    landing = jnp.zeros((ctx_size, query_heads, token_count), jnp.float32).at[sources].add(contrib)
    key_mass = lax.psum_scatter(landing, "ctx", scatter_dimension=0, tiled=True).reshape(
        query_heads, token_count
    )
    return (attn_out, key_mass)


def solution(mesh):
    in_specs = (P("ctx", "head", None), P("ctx", "head", None), P("ctx", "head", None), P(), P())
    out_specs = (P("ctx", "head", None), P("head", "ctx"))
    return jax.shard_map(
        on_device, mesh=mesh, in_specs=in_specs, out_specs=out_specs, check_vma=False
    )
```

profile of v0, /device:TPU:0, one launch (start us, length us, event | category | flops | bytes accessed | tf_op | source)
XLA Modules:
  0.0 163.1 jit_solution(17696914821971063014)
XLA Ops:
  7.2 1.2 gather_fusion.1
  8.5 1.3 gather_fusion
  9.8 1.1 maximum_bitcast_fusion
  11.9 7.3 %all-to-all-start = ((bf16[2,8,32,2,128]{4,2,3,0,1:T(8,128)(2,1)}), bf16[2,8,32,2,128]{4,2,3,0,1:T(8,128)(2,1)S(1)}, u32[]{:S(2)}, u32[]{:S(2)}) async-start(bf16[2,8,32,2,128]{4,2,3,0,1:T(8,128)(2,1)} %bitcast_select_fusion), calls=%async_computation | async-start | bytes 524288 | tf_op jit(solution)/shard_map/all_to_all | solution.py:44
  20.1 7.9 %all-to-all-done = bf16[2,8,32,2,128]{4,2,3,0,1:T(8,128)(2,1)S(1)} async-done(((bf16[2,8,32,2,128]{4,2,3,0,1:T(8,128)(2,1)}), bf16[2,8,32,2,128]{4,2,3,0,1:T(8,128)(2,1)S(1)}, u32[]{:S(2)}, u32[]{:S(2)}) %all-to-all-start) | async-done | bytes 262176 | tf_op jit(solution)/shard_map/all_to_all | solution.py:44
  28.9 1.5 collective-permute-start
  30.4 10.4 %collective-permute-done = bf16[2,16,32,2,128]{4,2,3,0,1:T(8,128)(2,1)S(1)} collective-permute-done((bf16[2,16,32,2,128]{4,2,3,0,1:T(8,128)(2,1)S(1)}, bf16[2,16,32,2,128]{4,2,3,0,1:T(8,128)(2,1)S(1)}, u32[]{:S(2)}, u32[]{:S(2)}) %collective-permute-start) | collective-permute-done | bytes 524320 | tf_op jit(solution)/shard_map/ppermute | solution.py:13
  43.4 1.2 copy.18
  44.6 18.8 %collective-permute-done.1 = bf16[2,16,64,2,128]{4,2,3,0,1:T(8,128)(2,1)S(1)} collective-permute-done((bf16[2,16,64,2,128]{4,2,3,0,1:T(8,128)(2,1)S(1)}, bf16[2,16,64,2,128]{4,2,3,0,1:T(8,128)(2,1)S(1)}, u32[]{:S(2)}, u32[]{:S(2)}) %collective-permute-start.1) | collective-permute-done | bytes 1048608 | tf_op jit(solution)/shard_map/ppermute | solution.py:13
  73.5 1.1 fusion.154
  79.8 1.0 fusion.33
  91.1 1.1 scatter_fusion
  92.9 2.5 %fusion.35 = bf16[128,16,128]{2,0,1:T(8,128)(2,1)} fusion(bf16[128,16,128]{2,0,1:T(8,128)(2,1)} %fusion.33, f32[128,2048]{0,1:T(8,128)} %copy-done.23, f32[128]{0:T(128)S(1)} %fusion.67, f32[128]{0:T(128)S(1)} %get-tuple-element.18, bf16[2,2,2048,128]{3,2,1,0:T(8,128)(2,1)} %bitcast.347), kind=kOutput, calls=%fused_computation.72 | convolution fusion | flops 67911680 | bytes 1606656 | tf_op jit(solution)/shard_map/dot_general | solution.py:89
  96.6 1.0 fusion.39
  99.1 1.0 fusion.43
  101.5 1.0 fusion.47
  104.0 1.0 fusion.51
  105.2 1.0 fusion.53
  106.5 1.0 fusion.55
  108.6 1.0 fusion.59
  109.6 1.0 fusion.61
  110.6 1.0 fusion.63
  111.5 2.2 %copy.19 = bf16[128,16,128]{2,1,0:T(8,128)(2,1)} copy(bf16[128,16,128]{2,0,1:T(8,128)(2,1)} %fusion.63) | data formatting | bytes 1048576
  113.7 42.6 %reduce-scatter.2.cloned.1.call-done = f32[1,16,128]{2,1,0:T(8,128)} async-done(((f32[8,16,128]{2,1,0:T(8,128)}), f32[1,16,128]{2,1,0:T(8,128)}) %reduce-scatter.2.cloned.1.call-update) | async-done | bytes 8208 | tf_op jit(solution)/shard_map/reduce_scatter | solution.py:102
  (143 shorter events, 38.9 us)
Async XLA Ops:
  11.9 16.2 %all-to-all-start = ((bf16[2,8,32,2,128]{4,2,3,0,1:T(8,128)(2,1)}), bf16[2,8,32,2,128]{4,2,3,0,1:T(8,128)(2,1)S(1)}, u32[]{:S(2)}, u32[]{:S(2)}) async-start(bf16[2,8,32,2,128]{4,2,3,0,1:T(8,128)(2,1)} %bitcast_select_fusion), calls=%async_computation | async-start | bytes 524288 | tf_op jit(solution)/shard_map/all_to_all | solution.py:44
  19.1 137.2 %reduce-scatter.2.cloned.1.call-start = ((), (), s32[]{:S(2)}) async-start(), calls=%async_computation.2 | async-start | bytes 73728 | tf_op jit(solution)/shard_map/reduce_scatter | solution.py:102
  28.1 13.8 %copy-start = (s32[2]{0:T(128)S(1)}, s32[2]{0:T(128)}, u32[]{:S(2)}) copy-start(s32[2]{0:T(128)} %param.9) | copy-start | bytes 28
  28.1 14.4 %copy-start.26 = (s32[2,4]{1,0:T(2,128)S(1)}, s32[2,4]{1,0:T(2,128)}, u32[]{:S(2)}) copy-start(s32[2,4]{1,0:T(2,128)} %param.8) | copy-start | bytes 100
  28.9 11.9 %collective-permute-start = (bf16[2,16,32,2,128]{4,2,3,0,1:T(8,128)(2,1)S(1)}, bf16[2,16,32,2,128]{4,2,3,0,1:T(8,128)(2,1)S(1)}, u32[]{:S(2)}, u32[]{:S(2)}) collective-permute-start(bf16[2,16,32,2,128]{4,2,3,0,1:T(8,128)(2,1)S(1)} %select_bitcast_fusion), channel_id=1, source_target_pairs={{0,4},{4,0},{8,12},{12,8},{16,20},{20,16},{24,28},{28,24},{1,5},{5... | collective-permute-start | bytes 1572872 | tf_op jit(solution)/shard_map/ppermute | solution.py:13
  41.1 22.2 %collective-permute-start.1 = (bf16[2,16,64,2,128]{4,2,3,0,1:T(8,128)(2,1)S(1)}, bf16[2,16,64,2,128]{4,2,3,0,1:T(8,128)(2,1)S(1)}, u32[]{:S(2)}, u32[]{:S(2)}) collective-permute-start(bf16[2,16,64,2,128]{4,2,3,0,1:T(8,128)(2,1)S(1)} %maximum_select_fusion.1), channel_id=1, source_target_pairs={{0,8},{4,12},{8,0},{12,4},{16,24},{20,28},{24,16},{28,20},{1,9},{5... | collective-permute-start | bytes 3145736 | tf_op jit(solution)/shard_map/ppermute | solution.py:13
  64.4 15.4 %copy-start.24 = (bf16[2,16,128,2,128]{4,2,1,3,0:T(8,128)(2,1)}, bf16[2,16,128,2,128]{4,2,1,3,0:T(8,128)(2,1)S(1)}, u32[]{:S(2)}) copy-start(bf16[2,16,128,2,128]{4,2,1,3,0:T(8,128)(2,1)S(1)} %copy.17) | copy-start | bytes 6291460
  68.0 15.0 %copy-start.1 = (f32[128,2048]{0,1:T(8,128)}, f32[128,2048]{0,1:T(8,128)S(1)}, u32[]{:S(2)}) copy-start(f32[128,2048]{0,1:T(8,128)S(1)} %get-tuple-element.41) | copy-start | bytes 3145732
  68.9 14.8 %copy-start.3 = (f32[128,2048]{0,1:T(8,128)}, f32[128,2048]{0,1:T(8,128)S(1)}, u32[]{:S(2)}) copy-start(f32[128,2048]{0,1:T(8,128)S(1)} %get-tuple-element.39) | copy-start | bytes 3145732
  69.8 14.5 %copy-start.5 = (f32[128,2048]{0,1:T(8,128)}, f32[128,2048]{0,1:T(8,128)S(1)}, u32[]{:S(2)}) copy-start(f32[128,2048]{0,1:T(8,128)S(1)} %get-tuple-element.37) | copy-start | bytes 3145732
  70.8 14.3 %copy-start.7 = (f32[128,2048]{0,1:T(8,128)}, f32[128,2048]{0,1:T(8,128)S(1)}, u32[]{:S(2)}) copy-start(f32[128,2048]{0,1:T(8,128)S(1)} %get-tuple-element.35) | copy-start | bytes 3145732
  71.7 14.0 %copy-start.9 = (f32[128,2048]{0,1:T(8,128)}, f32[128,2048]{0,1:T(8,128)S(1)}, u32[]{:S(2)}) copy-start(f32[128,2048]{0,1:T(8,128)S(1)} %get-tuple-element.33) | copy-start | bytes 3145732
  72.6 13.8 %copy-start.11 = (f32[128,2048]{0,1:T(8,128)}, f32[128,2048]{0,1:T(8,128)S(1)}, u32[]{:S(2)}) copy-start(f32[128,2048]{0,1:T(8,128)S(1)} %get-tuple-element.31) | copy-start | bytes 3145732
  73.5 13.5 %copy-start.13 = (f32[128,2048]{0,1:T(8,128)}, f32[128,2048]{0,1:T(8,128)S(1)}, u32[]{:S(2)}) copy-start(f32[128,2048]{0,1:T(8,128)S(1)} %get-tuple-element.29) | copy-start | bytes 3145732
  74.6 13.3 %copy-start.15 = (f32[128,2048]{0,1:T(8,128)}, f32[128,2048]{0,1:T(8,128)S(1)}, u32[]{:S(2)}) copy-start(f32[128,2048]{0,1:T(8,128)S(1)} %get-tuple-element.27) | copy-start | bytes 3145732
  75.5 13.0 %copy-start.17 = (f32[128,2048]{0,1:T(8,128)}, f32[128,2048]{0,1:T(8,128)S(1)}, u32[]{:S(2)}) copy-start(f32[128,2048]{0,1:T(8,128)S(1)} %get-tuple-element.25) | copy-start | bytes 3145732
  76.4 12.8 %copy-start.19 = (f32[128,2048]{0,1:T(8,128)}, f32[128,2048]{0,1:T(8,128)S(1)}, u32[]{:S(2)}) copy-start(f32[128,2048]{0,1:T(8,128)S(1)} %get-tuple-element.23) | copy-start | bytes 3145732
  77.3 12.5 %copy-start.21 = (f32[128,2048]{0,1:T(8,128)}, f32[128,2048]{0,1:T(8,128)S(1)}, u32[]{:S(2)}) copy-start(f32[128,2048]{0,1:T(8,128)S(1)} %get-tuple-element.21) | copy-start | bytes 3145732
  78.2 12.3 %copy-start.23 = (f32[128,2048]{0,1:T(8,128)}, f32[128,2048]{0,1:T(8,128)S(1)}, u32[]{:S(2)}) copy-start(f32[128,2048]{0,1:T(8,128)S(1)} %get-tuple-element.19) | copy-start | bytes 3145732
  92.9 2.5 %copy-start.22 = (f32[128,2048]{0,1:T(8,128)S(1)}, f32[128,2048]{0,1:T(8,128)}, u32[]{:S(2)}) copy-start(f32[128,2048]{0,1:T(8,128)} %copy-done.21) | copy-start | bytes 3145732
  92.9 2.5 %copy-start.25 = (bf16[2,16,128,2,128]{4,2,1,3,0:T(8,128)(2,1)S(1)}, bf16[2,16,128,2,128]{4,2,1,3,0:T(8,128)(2,1)}, u32[]{:S(2)}) copy-start(bf16[2,16,128,2,128]{4,2,1,3,0:T(8,128)(2,1)} %copy-done.24) | copy-start | bytes 6291460
  95.4 1.2 copy-start.20
  101.5 1.2 copy-start.10
  106.5 1.2 copy-start.2
  (8 other events, 9.2 us)
Sparse Core Ops, SparseCore 0:
  93.0 63.2 reduce-scatter.1
where the time goes:
time: 164 us; the launch traced here: 163 us
  waiting for transfers between devices  79.7 us (49%)
  matrix products  31.6 us (19%)
  other arithmetic  16.6 us (10%)
  between operations  14.5 us (9%)
  local copies, waits for them, and re-layouts  11.3 us (7%)
  starting transfers between devices  9.52 us (6%)
    reduce_scatter x1, waiting for transfers between devices, on_device(): lax.psum_scatter(landing, 'ctx', scatter_dimension=0, tiled=True)  42.6 us
    ppermute x2, waiting for transfers between devices, from_partner(): return lax.ppermute(value, axis, pairs)  29.2 us
    dot_general x16, matrix products, on_device(): jnp.dot(attention.astype(jnp.bfloat16), value_head, preferred_element_typ...  16.9 us
    dot_general x16, matrix products, on_device(): lax.dot_general(grouped[:, kv_head, group_index], key_head, contract_last...  14.7 us
    all_to_all x1, waiting for transfers between devices, on_device(): lax.all_to_all(outgoing, 'ctx', split_axis=1, concat_axis=1, tiled=True)  7.9 us
    all_to_all x1, starting transfers between devices, on_device(): lax.all_to_all(outgoing, 'ctx', split_axis=1, concat_axis=1, tiled=True)  7.28 us
    unnamed x63, local copies, waits for them, and re-layouts  6.8 us
    reduce_sum x16, other arithmetic, on_device(): head_masses.append(jnp.sum(attention, axis=0).reshape(slot_total, BLOCK))  5.65 us
  transfers between devices with their start and end apart: 4, of which 4 were waited for; matrix products, arithmetic and copies ran while one was open for 13% of the time, Pallas kernels for 0%

commit v1 on v0

--- a/solution.py
+++ b/solution.py
@@ -41,7 +41,21 @@
     )
     outgoing = outgoing.reshape(2, ctx_size, quarter, kv_total, head_depth)
     outgoing = jnp.where(wanted[None, :, None, None, None], outgoing, jnp.zeros((), outgoing.dtype))
-    incoming = lax.all_to_all(outgoing, "ctx", split_axis=1, concat_axis=1, tiled=True)
+    spare = lax.axis_size("ctx")
+    frame_out = lax.axis_index("ctx")
+    big, far_arr = (spare, frame_out)
+    mid_arr = outgoing.shape[1] // big
+    formed = list(outgoing.shape)
+    formed[1] = mid_arr
+    b_next = formed[1]
+    formed[1] = b_next * big
+    incoming = jnp.zeros(formed, outgoing.dtype)
+    for no in range(big):
+        y2 = lax.dynamic_slice_in_dim(outgoing, (far_arr ^ no) * mid_arr, mid_arr, axis=1)
+        if no:
+            right_arr = tuple(((it, it ^ no) for it in range(big)))
+            y2 = lax.ppermute(y2, "ctx", right_arr)
+        incoming = lax.dynamic_update_slice_in_dim(incoming, y2, (far_arr ^ no) * b_next, axis=1)
     sources = (listed[:, None] * split_count + jnp.arange(split_count)[None, :]).reshape(-1)
     fetched = jnp.take(incoming, sources, axis=1)
     bit_total = split_count.bit_length() - 1

time: 164 us -> 160 us (0.976)
  waiting for transfers between devices: 79.7 us -> 74.4 us
  starting transfers between devices: 9.52 us -> 13.3 us
    ppermute x0 -> x7, starting transfers between devices: none -> 12.6 us  [on_device(): y2 = lax.ppermute(y2, 'ctx', right_arr)]
    all_to_all x1 -> x0, waiting for transfers between devices: 7.9 us -> none  [on_device(): lax.all_to_all(outgoing, 'ctx', split_axis=1, concat_axis=1, tiled=True)]
    all_to_all x1 -> x0, starting transfers between devices: 7.28 us -> none  [on_device(): lax.all_to_all(outgoing, 'ctx', split_axis=1, concat_axis=1, tiled=True)]
    ppermute x0 -> x7, waiting for transfers between devices: none -> 6.51 us  [on_device(): y2 = lax.ppermute(y2, 'ctx', right_arr)]
    reduce_scatter x1, waiting for transfers between devices: 42.6 us -> 38.1 us  [on_device(): lax.psum_scatter(landing, 'ctx', scatter_dimension=0, tiled=True)]
    unnamed x63 -> x65, local copies, waits for them, and re-layouts: 6.8 us -> 5.79 us
  transfers between devices with their start and end apart: 4 -> 10, of which waited for: 4 -> 6; matrix products, arithmetic and copies ran while one was open for 13% -> 13% of each run, Pallas kernels for 0% -> 0%
where the time goes in v1:
time: 160 us
  waiting for transfers between devices  74.4 us (47%)
  matrix products  31.6 us (20%)
  other arithmetic  15.2 us (10%)
  between operations  14.7 us (9%)
  starting transfers between devices  13.3 us (8%)
  local copies, waits for them, and re-layouts  10.4 us (6%)
    reduce_scatter x1, waiting for transfers between devices, on_device(): lax.psum_scatter(landing, 'ctx', scatter_dimension=0, tiled=True)  38.1 us
    ppermute x2, waiting for transfers between devices, from_partner(): return lax.ppermute(value, axis, pairs)  29.8 us
    dot_general x16, matrix products, on_device(): jnp.dot(attention.astype(jnp.bfloat16), value_head, preferred_element_typ...  16.9 us
    dot_general x16, matrix products, on_device(): lax.dot_general(grouped[:, kv_head, group_index], key_head, contract_last...  14.7 us
    ppermute x7, starting transfers between devices, on_device(): y2 = lax.ppermute(y2, 'ctx', right_arr)  12.6 us
    ppermute x7, waiting for transfers between devices, on_device(): y2 = lax.ppermute(y2, 'ctx', right_arr)  6.51 us
    unnamed x65, local copies, waits for them, and re-layouts  5.79 us
    reduce_sum x16, other arithmetic, on_device(): head_masses.append(jnp.sum(attention, axis=0).reshape(slot_total, BLOCK))  5.65 us
  transfers between devices with their start and end apart: 10, of which 6 were waited for; matrix products, arithmetic and copies ran while one was open for 13% of the time, Pallas kernels for 0%

profile of v1, /device:TPU:0, one launch (start us, length us, event | category | flops | bytes accessed | tf_op | source)
XLA Modules:
  0.0 159.7 jit_solution(13690630826689850009)
XLA Ops:
  7.3 1.2 gather_fusion.1
  8.5 1.3 gather_fusion
  9.8 1.1 maximum_bitcast_fusion
  11.4 3.0 %collective-permute-start = (bf16[2,1,32,2,128]{4,2,3,1,0:T(8,128)(2,1)S(1)}, bf16[2,1,32,2,128]{4,2,3,1,0:T(8,128)(2,1)S(1)}, u32[]{:S(2)}, u32[]{:S(2)}) collective-permute-start(bf16[2,1,32,2,128]{4,2,3,1,0:T(8,128)(2,1)S(1)} %get-tuple-element.14), channel_id=1, source_target_pairs={{0,4},{4,0},{8,12},{12,8},{16,20},{20,16},{24,28},{28,24},{1,5},{5... | collective-permute-start | bytes 98312 | tf_op jit(solution)/shard_map/ppermute | solution.py:57
  14.5 1.6 collective-permute-start.1
  16.0 3.0 %collective-permute-start.3 = (bf16[2,1,32,2,128]{4,2,3,1,0:T(8,128)(2,1)S(1)}, bf16[2,1,32,2,128]{4,2,3,1,0:T(8,128)(2,1)S(1)}, u32[]{:S(2)}, u32[]{:S(2)}) collective-permute-start(bf16[2,1,32,2,128]{4,2,3,1,0:T(8,128)(2,1)S(1)} %get-tuple-element.11), channel_id=1, source_target_pairs={{0,16},{4,20},{8,24},{12,28},{16,0},{20,4},{24,8},{28,12},{1,17},{... | collective-permute-start | bytes 98312 | tf_op jit(solution)/shard_map/ppermute | solution.py:57
  19.0 1.3 collective-permute-start.4
  20.6 3.7 %collective-permute-start.5 = (bf16[2,1,32,2,128]{4,2,3,1,0:T(8,128)(2,1)S(1)}, bf16[2,1,32,2,128]{4,2,3,1,0:T(8,128)(2,1)S(1)}, u32[]{:S(2)}, u32[]{:S(2)}) collective-permute-start(bf16[2,1,32,2,128]{4,2,3,1,0:T(8,128)(2,1)S(1)} %get-tuple-element.9), channel_id=1, source_target_pairs={{0,24},{4,28},{8,16},{12,20},{16,8},{20,12},{24,0},{28,4},{1,25},{... | collective-permute-start | bytes 98312 | tf_op jit(solution)/shard_map/ppermute | solution.py:57
  24.7 1.6 %collective-permute-done.5 = bf16[2,1,32,2,128]{4,2,3,1,0:T(8,128)(2,1)S(1)} collective-permute-done((bf16[2,1,32,2,128]{4,2,3,1,0:T(8,128)(2,1)S(1)}, bf16[2,1,32,2,128]{4,2,3,1,0:T(8,128)(2,1)S(1)}, u32[]{:S(2)}, u32[]{:S(2)}) %collective-permute-start.5) | collective-permute-done | bytes 32800 | tf_op jit(solution)/shard_map/ppermute | solution.py:57
  26.4 4.6 %collective-permute-done.6 = bf16[2,1,32,2,128]{4,2,3,1,0:T(8,128)(2,1)S(1)} collective-permute-done((bf16[2,1,32,2,128]{4,2,3,1,0:T(8,128)(2,1)S(1)}, bf16[2,1,32,2,128]{4,2,3,1,0:T(8,128)(2,1)S(1)}, u32[]{:S(2)}, u32[]{:S(2)}) %collective-permute-start.6) | collective-permute-done | bytes 32800 | tf_op jit(solution)/shard_map/ppermute | solution.py:57
  32.3 10.4 %collective-permute-done.7 = bf16[2,16,32,2,128]{4,2,3,0,1:T(8,128)(2,1)S(1)} collective-permute-done((bf16[2,16,32,2,128]{4,2,3,0,1:T(8,128)(2,1)S(1)}, bf16[2,16,32,2,128]{4,2,3,0,1:T(8,128)(2,1)S(1)}, u32[]{:S(2)}, u32[]{:S(2)}) %collective-permute-start.7) | collective-permute-done | bytes 524320 | tf_op jit(solution)/shard_map/ppermute | solution.py:13
  44.9 19.5 %collective-permute-done.8 = bf16[2,16,64,2,128]{4,2,3,0,1:T(8,128)(2,1)S(1)} collective-permute-done((bf16[2,16,64,2,128]{4,2,3,0,1:T(8,128)(2,1)S(1)}, bf16[2,16,64,2,128]{4,2,3,0,1:T(8,128)(2,1)S(1)}, u32[]{:S(2)}, u32[]{:S(2)}) %collective-permute-start.8) | collective-permute-done | bytes 1048608 | tf_op jit(solution)/shard_map/ppermute | solution.py:13
  73.6 1.1 fusion.155
  92.1 1.1 scatter_fusion
  94.0 2.5 %fusion.35 = bf16[128,16,128]{2,0,1:T(8,128)(2,1)} fusion(bf16[128,16,128]{2,0,1:T(8,128)(2,1)} %fusion.33, f32[128,2048]{0,1:T(8,128)} %copy-done.23, f32[128]{0:T(128)S(1)} %fusion.67, f32[128]{0:T(128)S(1)} %get-tuple-element.24, bf16[2,2,2048,128]{3,2,1,0:T(8,128)(2,1)} %bitcast.346), kind=kOutput, calls=%fused_computation.72 | convolution fusion | flops 67911680 | bytes 1606656 | tf_op jit(solution)/shard_map/dot_general | solution.py:103
  100.1 1.0 fusion.43
  102.6 1.0 fusion.47
  105.0 1.0 fusion.51
  107.5 1.0 fusion.55
  109.7 1.0 fusion.59
  110.7 1.0 fusion.61
  111.6 1.0 fusion.63
  112.6 2.2 %copy.14 = bf16[128,16,128]{2,1,0:T(8,128)(2,1)} copy(bf16[128,16,128]{2,0,1:T(8,128)(2,1)} %fusion.63) | data formatting | bytes 1048576
  114.8 38.1 %reduce-scatter.2.cloned.1.call-done = f32[1,16,128]{2,1,0:T(8,128)} async-done(((f32[8,16,128]{2,1,0:T(8,128)}), f32[1,16,128]{2,1,0:T(8,128)}) %reduce-scatter.2.cloned.1.call-update) | async-done | bytes 8208 | tf_op jit(solution)/shard_map/reduce_scatter | solution.py:116
  (166 shorter events, 41.1 us)
Async XLA Ops:
  7.2 13.2 %copy-start.26 = (s32[2,4]{1,0:T(2,128)S(1)}, s32[2,4]{1,0:T(2,128)}, u32[]{:S(2)}) copy-start(s32[2,4]{1,0:T(2,128)} %param.8) | copy-start | bytes 100
  7.2 145.7 %reduce-scatter.2.cloned.1.call-start = ((), (), s32[]{:S(2)}) async-start(), calls=%async_computation.1 | async-start | bytes 73728 | tf_op jit(solution)/shard_map/reduce_scatter | solution.py:116
  11.4 9.2 %collective-permute-start = (bf16[2,1,32,2,128]{4,2,3,1,0:T(8,128)(2,1)S(1)}, bf16[2,1,32,2,128]{4,2,3,1,0:T(8,128)(2,1)S(1)}, u32[]{:S(2)}, u32[]{:S(2)}) collective-permute-start(bf16[2,1,32,2,128]{4,2,3,1,0:T(8,128)(2,1)S(1)} %get-tuple-element.14), channel_id=1, source_target_pairs={{0,4},{4,0},{8,12},{12,8},{16,20},{20,16},{24,28},{28,24},{1,5},{5... | collective-permute-start | bytes 98312 | tf_op jit(solution)/shard_map/ppermute | solution.py:57
  14.5 9.8 %collective-permute-start.1 = (bf16[2,1,32,2,128]{4,2,3,1,0:T(8,128)(2,1)S(1)}, bf16[2,1,32,2,128]{4,2,3,1,0:T(8,128)(2,1)S(1)}, u32[]{:S(2)}, u32[]{:S(2)}) collective-permute-start(bf16[2,1,32,2,128]{4,2,3,1,0:T(8,128)(2,1)S(1)} %get-tuple-element.13), channel_id=1, source_target_pairs={{0,8},{4,12},{8,0},{12,4},{16,24},{20,28},{24,16},{28,20},{1,9},{5... | collective-permute-start | bytes 98312 | tf_op jit(solution)/shard_map/ppermute | solution.py:57
  16.0 8.3 %collective-permute-start.2 = (bf16[2,1,32,2,128]{4,2,3,1,0:T(8,128)(2,1)S(1)}, bf16[2,1,32,2,128]{4,2,3,1,0:T(8,128)(2,1)S(1)}, u32[]{:S(2)}, u32[]{:S(2)}) collective-permute-start(bf16[2,1,32,2,128]{4,2,3,1,0:T(8,128)(2,1)S(1)} %get-tuple-element.12), channel_id=1, source_target_pairs={{0,12},{4,8},{8,4},{12,0},{16,28},{20,24},{24,20},{28,16},{1,13},{... | collective-permute-start | bytes 98312 | tf_op jit(solution)/shard_map/ppermute | solution.py:57
  16.0 8.4 %collective-permute-start.3 = (bf16[2,1,32,2,128]{4,2,3,1,0:T(8,128)(2,1)S(1)}, bf16[2,1,32,2,128]{4,2,3,1,0:T(8,128)(2,1)S(1)}, u32[]{:S(2)}, u32[]{:S(2)}) collective-permute-start(bf16[2,1,32,2,128]{4,2,3,1,0:T(8,128)(2,1)S(1)} %get-tuple-element.11), channel_id=1, source_target_pairs={{0,16},{4,20},{8,24},{12,28},{16,0},{20,4},{24,8},{28,12},{1,17},{... | collective-permute-start | bytes 98312 | tf_op jit(solution)/shard_map/ppermute | solution.py:57
  19.0 5.7 %collective-permute-start.4 = (bf16[2,1,32,2,128]{4,2,3,1,0:T(8,128)(2,1)S(1)}, bf16[2,1,32,2,128]{4,2,3,1,0:T(8,128)(2,1)S(1)}, u32[]{:S(2)}, u32[]{:S(2)}) collective-permute-start(bf16[2,1,32,2,128]{4,2,3,1,0:T(8,128)(2,1)S(1)} %get-tuple-element.10), channel_id=1, source_target_pairs={{0,20},{4,16},{8,28},{12,24},{16,4},{20,0},{24,12},{28,8},{1,21},{... | collective-permute-start | bytes 98312 | tf_op jit(solution)/shard_map/ppermute | solution.py:57
  20.6 5.8 %collective-permute-start.5 = (bf16[2,1,32,2,128]{4,2,3,1,0:T(8,128)(2,1)S(1)}, bf16[2,1,32,2,128]{4,2,3,1,0:T(8,128)(2,1)S(1)}, u32[]{:S(2)}, u32[]{:S(2)}) collective-permute-start(bf16[2,1,32,2,128]{4,2,3,1,0:T(8,128)(2,1)S(1)} %get-tuple-element.9), channel_id=1, source_target_pairs={{0,24},{4,28},{8,16},{12,20},{16,8},{20,12},{24,0},{28,4},{1,25},{... | collective-permute-start | bytes 98312 | tf_op jit(solution)/shard_map/ppermute | solution.py:57
  24.3 6.7 %collective-permute-start.6 = (bf16[2,1,32,2,128]{4,2,3,1,0:T(8,128)(2,1)S(1)}, bf16[2,1,32,2,128]{4,2,3,1,0:T(8,128)(2,1)S(1)}, u32[]{:S(2)}, u32[]{:S(2)}) collective-permute-start(bf16[2,1,32,2,128]{4,2,3,1,0:T(8,128)(2,1)S(1)} %get-tuple-element.8), channel_id=1, source_target_pairs={{0,28},{4,24},{8,20},{12,16},{16,12},{20,8},{24,4},{28,0},{1,29},{... | collective-permute-start | bytes 98312 | tf_op jit(solution)/shard_map/ppermute | solution.py:57
  31.0 13.8 %copy-start.28 = (bf16[128,16,128]{2,1,0:T(8,128)(2,1)S(1)}, bf16[128,16,128]{2,1,0:T(8,128)(2,1)}, u32[]{:S(2)}) copy-start(bf16[128,16,128]{2,1,0:T(8,128)(2,1)} %param.5) | copy-start | bytes 1572868
  31.8 10.9 %collective-permute-start.7 = (bf16[2,16,32,2,128]{4,2,3,0,1:T(8,128)(2,1)S(1)}, bf16[2,16,32,2,128]{4,2,3,0,1:T(8,128)(2,1)S(1)}, u32[]{:S(2)}, u32[]{:S(2)}) collective-permute-start(bf16[2,16,32,2,128]{4,2,3,0,1:T(8,128)(2,1)S(1)} %select_bitcast_fusion), channel_id=1, source_target_pairs={{0,4},{4,0},{8,12},{12,8},{16,20},{20,16},{24,28},{28,24},{1,5},{5... | collective-permute-start | bytes 1572872 | tf_op jit(solution)/shard_map/ppermute | solution.py:13
  43.1 21.2 %collective-permute-start.8 = (bf16[2,16,64,2,128]{4,2,3,0,1:T(8,128)(2,1)S(1)}, bf16[2,16,64,2,128]{4,2,3,0,1:T(8,128)(2,1)S(1)}, u32[]{:S(2)}, u32[]{:S(2)}) collective-permute-start(bf16[2,16,64,2,128]{4,2,3,0,1:T(8,128)(2,1)S(1)} %maximum_select_fusion.1), channel_id=1, source_target_pairs={{0,8},{4,12},{8,0},{12,4},{16,24},{20,28},{24,16},{28,20},{1,9},{5... | collective-permute-start | bytes 3145736 | tf_op jit(solution)/shard_map/ppermute | solution.py:13
  65.4 15.4 %copy-start.24 = (bf16[2,16,128,2,128]{4,2,1,3,0:T(8,128)(2,1)}, bf16[2,16,128,2,128]{4,2,1,3,0:T(8,128)(2,1)S(1)}, u32[]{:S(2)}) copy-start(bf16[2,16,128,2,128]{4,2,1,3,0:T(8,128)(2,1)S(1)} %copy.12) | copy-start | bytes 6291460
  69.0 15.0 %copy-start.1 = (f32[128,2048]{0,1:T(8,128)}, f32[128,2048]{0,1:T(8,128)S(1)}, u32[]{:S(2)}) copy-start(f32[128,2048]{0,1:T(8,128)S(1)} %get-tuple-element.47) | copy-start | bytes 3145732
  70.0 14.8 %copy-start.3 = (f32[128,2048]{0,1:T(8,128)}, f32[128,2048]{0,1:T(8,128)S(1)}, u32[]{:S(2)}) copy-start(f32[128,2048]{0,1:T(8,128)S(1)} %get-tuple-element.45) | copy-start | bytes 3145732
  70.9 14.5 %copy-start.5 = (f32[128,2048]{0,1:T(8,128)}, f32[128,2048]{0,1:T(8,128)S(1)}, u32[]{:S(2)}) copy-start(f32[128,2048]{0,1:T(8,128)S(1)} %get-tuple-element.43) | copy-start | bytes 3145732
  71.8 14.3 %copy-start.7 = (f32[128,2048]{0,1:T(8,128)}, f32[128,2048]{0,1:T(8,128)S(1)}, u32[]{:S(2)}) copy-start(f32[128,2048]{0,1:T(8,128)S(1)} %get-tuple-element.41) | copy-start | bytes 3145732
  72.7 14.0 %copy-start.9 = (f32[128,2048]{0,1:T(8,128)}, f32[128,2048]{0,1:T(8,128)S(1)}, u32[]{:S(2)}) copy-start(f32[128,2048]{0,1:T(8,128)S(1)} %get-tuple-element.39) | copy-start | bytes 3145732
  73.6 14.0 %copy-start.11 = (f32[128,2048]{0,1:T(8,128)}, f32[128,2048]{0,1:T(8,128)S(1)}, u32[]{:S(2)}) copy-start(f32[128,2048]{0,1:T(8,128)S(1)} %get-tuple-element.37) | copy-start | bytes 3145732
  74.7 13.5 %copy-start.13 = (f32[128,2048]{0,1:T(8,128)}, f32[128,2048]{0,1:T(8,128)S(1)}, u32[]{:S(2)}) copy-start(f32[128,2048]{0,1:T(8,128)S(1)} %get-tuple-element.35) | copy-start | bytes 3145732
  75.6 13.3 %copy-start.15 = (f32[128,2048]{0,1:T(8,128)}, f32[128,2048]{0,1:T(8,128)S(1)}, u32[]{:S(2)}) copy-start(f32[128,2048]{0,1:T(8,128)S(1)} %get-tuple-element.33) | copy-start | bytes 3145732
  76.5 13.0 %copy-start.17 = (f32[128,2048]{0,1:T(8,128)}, f32[128,2048]{0,1:T(8,128)S(1)}, u32[]{:S(2)}) copy-start(f32[128,2048]{0,1:T(8,128)S(1)} %get-tuple-element.31) | copy-start | bytes 3145732
  77.4 12.8 %copy-start.19 = (f32[128,2048]{0,1:T(8,128)}, f32[128,2048]{0,1:T(8,128)S(1)}, u32[]{:S(2)}) copy-start(f32[128,2048]{0,1:T(8,128)S(1)} %get-tuple-element.29) | copy-start | bytes 3145732
  78.3 12.5 %copy-start.21 = (f32[128,2048]{0,1:T(8,128)}, f32[128,2048]{0,1:T(8,128)S(1)}, u32[]{:S(2)}) copy-start(f32[128,2048]{0,1:T(8,128)S(1)} %get-tuple-element.27) | copy-start | bytes 3145732
  (15 other events, 42.4 us)
Sparse Core Ops, SparseCore 0:
  94.1 58.7 reduce-scatter.1
